TPU v7x, 32 devices: a whole 2x2x4 slice. The times are simulated.
32 devices in a mesh: expert: 8 (over y, x, core), shard: 4 (over z).
Axes of the slice: x: 2, y: 2, z: 4, core: 2. Of those that a mesh axis runs over, the one named last changes fastest.
Arguments:
- block_input: float32 [64, 65, 768], P(('expert', 'shard')), may hold values from -6 to 6
- image_live: int32 [64], P(('expert', 'shard')), may hold values from 0 to 1, as said below
- expert_routes: int32 [64, 65, 2], P(('expert', 'shard')), may hold values from 0 to 7, all different within a row; in each aligned block of 130 rows (0 to 129, 130 to 259, ..., all dimensions but the last counted through in order) at most 49 rows name the same one
- first_gain: bfloat16 [768], P('shard'), may hold values from 0.5 to 1.5
- first_shift: bfloat16 [768], P('shard'), may hold values from -3 to 3
- qkv_weight: bfloat16 [768, 2304], P('shard'), may hold values from -0.21875 to 0.21875
- query_value_bias: bfloat16 [1536], P('shard'), may hold values from -2 to 2
- attn_out_weight: bfloat16 [768, 768], P('shard'), may hold values from -0.4375 to 0.4375
- attn_out_bias: bfloat16 [768], P('shard'), may hold values from -3 to 3
- second_gain: bfloat16 [768], P('shard'), may hold values from 0.5 to 1.5
- second_shift: bfloat16 [768], P('shard'), may hold values from -3 to 3
- router_weight: bfloat16 [768, 8], P('shard'), may hold values from -0.28867513 to 0.28867513
- expert_in_weight: bfloat16 [8, 768, 3072], P('expert', None, 'shard'), may hold values from -0.21875 to 0.21875
- expert_in_bias: bfloat16 [8, 3072], P('expert', 'shard'), may hold values from -3 to 3
- expert_out_weight: bfloat16 [8, 3072, 768], P('expert', None, 'shard'), may hold values from -1.75 to 1.75
- expert_out_bias: bfloat16 [8, 768], P('expert', 'shard'), may hold values from -5 to 5
- output_grad: float32 [64, 65, 768], P(('expert', 'shard')), may hold values from -6 to 6
Outputs:
- block_output: float32 [64, 65, 768], P(('expert', 'shard'))
- input_grad: float32 [64, 65, 768], P(('expert', 'shard'))
- first_gain_grad: float32 [768], P('shard')
- first_shift_grad: float32 [768], P('shard')
- qkv_weight_grad: float32 [768, 2304], P('shard')
- query_value_bias_grad: float32 [1536], P('shard')
- attn_out_weight_grad: float32 [768, 768], P('shard')
- attn_out_bias_grad: float32 [768], P('shard')
- second_gain_grad: float32 [768], P('shard')
- second_shift_grad: float32 [768], P('shard')
- router_weight_grad: float32 [768, 8], P('shard')
- expert_in_weight_grad: float32 [8, 768, 3072], P('expert', None, 'shard')
- expert_in_bias_grad: float32 [8, 3072], P('expert', 'shard')
- expert_out_weight_grad: float32 [8, 3072, 768], P('expert', None, 'shard')
- expert_out_bias_grad: float32 [8, 768], P('expert', 'shard')
Inputs may be any that keep to these rules, and one draw needn't show every extreme that they name: `expert_routes`: each token names two different experts; among the rows of the image slots i with i // 2 equal, no expert is named more than 49 times, a bound that some block reaches. image_live[i] is 1 wherever i is a multiple of 2.
All inputs are finite; a program needn't handle non-finite values.
Results may differ from a plain program's by a relative error of at most 0.023.
Values may be sent and summed in bfloat16 or wider, within the bound.
A program may use at most 128 MiB of HBM per device.

v0:
```python
import math

import jax
import jax.numpy as jnp
from jax import lax
from jax.sharding import PartitionSpec as P

HEADS = 12
HEAD_DIM = 64


EPSILON = 1e-06
PRECISE = lax.Precision.HIGHEST
HALF_ROOT = 0.7071067811865476
DENSITY = 0.3989422804014327


def as_float(array_in):
    return array_in.astype(jnp.float32)


def contract_rows(left_side, right_side):
    return lax.dot_general(
        left_side, right_side, (((0,), (0,)), ((), ())), preferred_element_type=jnp.float32
    )


def contract_cols(left_side, right_side):
    return lax.dot_general(
        left_side, right_side, (((1,), (1,)), ((), ())), preferred_element_type=jnp.float32
    )


def precise_rows(left_side, right_side):
    return lax.dot_general(
        left_side,
        right_side,
        (((0,), (0,)), ((), ())),
        precision=PRECISE,
        preferred_element_type=jnp.float32,
    )


def precise_cols(left_side, right_side):
    return lax.dot_general(
        left_side,
        right_side,
        (((1,), (1,)), ((), ())),
        precision=PRECISE,
        preferred_element_type=jnp.float32,
    )


def layer_norm(values_in, gain_vec, shift_vec):
    center = values_in - jnp.mean(values_in, axis=-1, keepdims=True)
    inv_std = lax.rsqrt(jnp.mean(center * center, axis=-1, keepdims=True) + EPSILON)
    normed = center * inv_std
    return (normed * as_float(gain_vec) + as_float(shift_vec), normed, inv_std)


def norm_back(upstream, normed, inv_std, gain_vec):
    scaled = upstream * as_float(gain_vec)
    return inv_std * (
        scaled
        - jnp.mean(scaled, axis=-1, keepdims=True)
        - normed * jnp.mean(scaled * normed, axis=-1, keepdims=True)
    )


def gelu_parts(pre_act):
    normal_cdf = 0.5 * (1.0 + jax.scipy.special.erf(pre_act * HALF_ROOT))
    return (
        pre_act * normal_cdf,
        normal_cdf + pre_act * DENSITY * jnp.exp(-0.5 * pre_act * pre_act),
    )


def route_tables(expert_routes, image_live, expert_count, capacity):
    row_count = expert_routes.shape[0] * expert_routes.shape[1]
    flat_routes = expert_routes.reshape(2 * row_count)
    live_rows = jnp.repeat(image_live, expert_routes.shape[1])
    alive_pairs = jnp.repeat(live_rows, 2)
    chosen = (flat_routes[:, None] == jnp.arange(expert_count, dtype=jnp.int32)[None, :]).astype(
        jnp.int32
    )
    live_hits = chosen * alive_pairs[:, None]
    position = jnp.sum(
        (jnp.cumsum(live_hits, axis=0, dtype=jnp.int32) - live_hits) * live_hits,
        axis=1,
        dtype=jnp.int32,
    )
    slot_index = flat_routes * capacity + position
    slot_table = (
        (slot_index[None, :] == jnp.arange(expert_count * capacity, dtype=jnp.int32)[:, None])
        & (alive_pairs[None, :] > 0)
    ).astype(jnp.bfloat16)
    return (chosen.reshape(row_count, 2, expert_count), slot_table, live_rows)


def attention_scores(query_rows, key_rows):
    return jnp.einsum(
        "bqhd,bkhd->bhqk", query_rows, key_rows, preferred_element_type=jnp.float32
    ) * (1.0 / math.sqrt(HEAD_DIM))


def body(
    block_input,
    image_live,
    expert_routes,
    first_gain,
    first_shift,
    qkv_weight,
    query_value_bias,
    attn_out_weight,
    attn_out_bias,
    second_gain,
    second_shift,
    router_weight,
    expert_in_weight,
    expert_in_bias,
    expert_out_weight,
    expert_out_bias,
    output_grad,
):
    image_count, seq_length, model_width = block_input.shape
    row_count = image_count * seq_length
    (
        gain_one,
        shift_one,
        qkv_full,
        bias_full,
        proj_full,
        proj_bias,
        gain_two,
        shift_two,
        router_full,
    ) = (
        lax.all_gather(first_gain, "shard", axis=0, tiled=True),
        lax.all_gather(first_shift, "shard", axis=0, tiled=True),
        lax.all_gather(qkv_weight, "shard", axis=0, tiled=True),
        lax.all_gather(query_value_bias, "shard", axis=0, tiled=True),
        lax.all_gather(attn_out_weight, "shard", axis=0, tiled=True),
        lax.all_gather(attn_out_bias, "shard", axis=0, tiled=True),
        lax.all_gather(second_gain, "shard", axis=0, tiled=True),
        lax.all_gather(second_shift, "shard", axis=0, tiled=True),
        lax.all_gather(router_weight, "shard", axis=0, tiled=True),
    )
    in_stack, in_bias_stack, out_stack, out_bias_stack = (
        lax.all_gather(expert_in_weight, "shard", axis=2, tiled=True),
        lax.all_gather(expert_in_bias, "shard", axis=1, tiled=True),
        lax.all_gather(expert_out_weight, "shard", axis=2, tiled=True),
        lax.all_gather(expert_out_bias, "shard", axis=1, tiled=True),
    )
    in_full = in_stack[0]
    in_bias_full = in_bias_stack[0]
    out_full = out_stack[0]
    out_bias_full = out_bias_stack[0]
    flat_tokens = block_input.reshape(row_count, model_width)
    norm_out, normed_one, inv_one = layer_norm(flat_tokens, gain_one, shift_one)
    attn_in = norm_out.astype(jnp.bfloat16)
    bias_row = jnp.concatenate(
        [
            as_float(bias_full[:model_width]),
            jnp.zeros((model_width,), jnp.float32),
            as_float(bias_full[model_width:]),
        ]
    )
    packed = (
        (jnp.dot(attn_in, qkv_full, preferred_element_type=jnp.float32) + bias_row)
        .astype(jnp.bfloat16)
        .reshape(image_count, seq_length, 3, HEADS, HEAD_DIM)
    )
    query_rows = packed[:, :, 0]
    key_rows = packed[:, :, 1]
    value_rows = packed[:, :, 2]
    scores = attention_scores(query_rows, key_rows)
    row_max = jnp.max(scores, axis=-1, keepdims=True)
    log_total = row_max + jnp.log(jnp.sum(jnp.exp(scores - row_max), axis=-1, keepdims=True))
    weights = jnp.exp(scores - log_total).astype(jnp.bfloat16)
    mixed_heads = (
        jnp.einsum("bhqk,bkhd->bqhd", weights, value_rows, preferred_element_type=jnp.float32)
        .astype(jnp.bfloat16)
        .reshape(row_count, model_width)
    )
    residual = (
        flat_tokens
        + jnp.dot(mixed_heads, proj_full, preferred_element_type=jnp.float32)
        + as_float(proj_bias)
    )
    norm_two_out, normed_two, inv_two = layer_norm(residual, gain_two, shift_two)
    expert_in = norm_two_out.astype(jnp.bfloat16)
    logits = jnp.dot(expert_in, router_full, preferred_element_type=jnp.float32)
    shifted = jnp.exp(logits - jnp.max(logits, axis=-1, keepdims=True))
    gate_probs = shifted / jnp.sum(shifted, axis=-1, keepdims=True)
    expert_count = router_full.shape[1]
    capacity = (3 * row_count + expert_count - 1) // expert_count
    chosen, slot_table, live_rows = route_tables(expert_routes, image_live, expert_count, capacity)
    gate_pick = jnp.sum(gate_probs[:, None, :] * as_float(chosen), axis=2)
    send_table = jnp.sum(slot_table.reshape(expert_count * capacity, row_count, 2), axis=2)
    outgoing = (
        jnp.dot(send_table, expert_in, preferred_element_type=jnp.float32)
        .astype(jnp.bfloat16)
        .reshape(expert_count, capacity, model_width)
    )
    incoming = lax.all_to_all(outgoing, "expert", split_axis=0, concat_axis=0, tiled=True).reshape(
        expert_count * capacity, model_width
    )
    pre_act = jnp.dot(incoming, in_full, preferred_element_type=jnp.float32) + as_float(
        in_bias_full
    )
    gelu_out, gelu_slope = gelu_parts(pre_act)
    gelu_bf = gelu_out.astype(jnp.bfloat16)
    expert_out = (
        jnp.dot(gelu_bf, out_full, preferred_element_type=jnp.float32) + as_float(out_bias_full)
    ).astype(jnp.bfloat16)
    returned = lax.all_to_all(
        expert_out.reshape(expert_count, capacity, model_width),
        "expert",
        split_axis=0,
        concat_axis=0,
        tiled=True,
    ).reshape(expert_count * capacity, model_width)
    picked = contract_rows(slot_table, returned).reshape(row_count, 2, model_width)
    live_col = as_float(live_rows)[:, None]
    block_output = residual + live_col * jnp.sum(gate_pick[:, :, None] * picked, axis=1)
    upstream = output_grad.reshape(row_count, model_width) * live_col
    gate_grad = jnp.sum(upstream[:, None, :] * picked, axis=2)
    sent_grad = (
        (gate_pick[:, :, None] * upstream[:, None, :])
        .astype(jnp.bfloat16)
        .reshape(2 * row_count, model_width)
    )
    grad_out = (
        jnp.dot(slot_table, sent_grad, preferred_element_type=jnp.float32)
        .astype(jnp.bfloat16)
        .reshape(expert_count, capacity, model_width)
    )
    grad_in = lax.all_to_all(grad_out, "expert", split_axis=0, concat_axis=0, tiled=True).reshape(
        expert_count * capacity, model_width
    )
    gain_back_one, qkv_back, proj_back, gain_back_two, router_back = (
        lax.all_gather(first_gain, "shard", axis=0, tiled=True),
        lax.all_gather(qkv_weight, "shard", axis=0, tiled=True),
        lax.all_gather(attn_out_weight, "shard", axis=0, tiled=True),
        lax.all_gather(second_gain, "shard", axis=0, tiled=True),
        lax.all_gather(router_weight, "shard", axis=0, tiled=True),
    )
    in_again, out_again = (
        lax.all_gather(expert_in_weight, "shard", axis=2, tiled=True),
        lax.all_gather(expert_out_weight, "shard", axis=2, tiled=True),
    )
    in_back = in_again[0]
    out_back = out_again[0]
    out_bias_grad = jnp.sum(as_float(grad_in), axis=0)
    out_weight_grad = contract_rows(gelu_bf, grad_in)
    pre_grad = contract_cols(grad_in, out_back) * gelu_slope
    in_bias_grad = jnp.sum(pre_grad, axis=0)
    pre_bf = pre_grad.astype(jnp.bfloat16)
    back_rows = contract_cols(pre_bf, in_back).astype(jnp.bfloat16)
    returned_grad = lax.all_to_all(
        back_rows.reshape(expert_count, capacity, model_width),
        "expert",
        split_axis=0,
        concat_axis=0,
        tiled=True,
    ).reshape(expert_count * capacity, model_width)
    in_weight_grad = contract_rows(incoming, pre_bf)
    in_weight_part, in_bias_part, out_weight_part, out_bias_part = (
        lax.psum_scatter(
            in_weight_grad[None].astype(jnp.bfloat16), "shard", scatter_dimension=2, tiled=True
        ).astype(jnp.float32),
        lax.psum_scatter(
            in_bias_grad[None].astype(jnp.bfloat16), "shard", scatter_dimension=1, tiled=True
        ).astype(jnp.float32),
        lax.psum_scatter(
            out_weight_grad[None].astype(jnp.bfloat16), "shard", scatter_dimension=2, tiled=True
        ).astype(jnp.float32),
        lax.psum_scatter(
            out_bias_grad[None].astype(jnp.bfloat16), "shard", scatter_dimension=1, tiled=True
        ).astype(jnp.float32),
    )
    full_gate_grad = jnp.sum(gate_grad[:, :, None] * as_float(chosen), axis=1)
    logit_grad = gate_probs * (
        full_gate_grad - jnp.sum(gate_probs * full_gate_grad, axis=-1, keepdims=True)
    )
    router_grad = precise_rows(as_float(expert_in), logit_grad)
    route_grad = jnp.sum(
        contract_rows(slot_table, returned_grad).reshape(row_count, 2, model_width), axis=1
    )
    normed_two_grad = route_grad + precise_cols(logit_grad, as_float(router_back))
    second_gain_grad = jnp.sum(normed_two_grad * normed_two, axis=0)
    second_shift_grad = jnp.sum(normed_two_grad, axis=0)
    residual_grad = upstream + norm_back(normed_two_grad, normed_two, inv_two, gain_back_two)
    proj_bias_grad = jnp.sum(residual_grad, axis=0)
    residual_bf = residual_grad.astype(jnp.bfloat16)
    proj_grad = contract_rows(mixed_heads, residual_bf)
    mixed_grad = (
        contract_cols(residual_bf, proj_back)
        .astype(jnp.bfloat16)
        .reshape(image_count, seq_length, HEADS, HEAD_DIM)
    )
    scores_again = attention_scores(query_rows, key_rows)
    probs = jnp.exp(scores_again - log_total)
    probs_bf = probs.astype(jnp.bfloat16)
    value_grad = jnp.einsum(
        "bhqk,bqhd->bkhd", probs_bf, mixed_grad, preferred_element_type=jnp.float32
    )
    prob_grad = jnp.einsum(
        "bqhd,bkhd->bhqk", mixed_grad, value_rows, preferred_element_type=jnp.float32
    )
    score_grad = (
        probs
        * (prob_grad - jnp.sum(probs * prob_grad, axis=-1, keepdims=True))
        * (1.0 / math.sqrt(HEAD_DIM))
    ).astype(jnp.bfloat16)
    query_grad = jnp.einsum(
        "bhqk,bkhd->bqhd", score_grad, key_rows, preferred_element_type=jnp.float32
    )
    key_grad = jnp.einsum(
        "bhqk,bqhd->bkhd", score_grad, query_rows, preferred_element_type=jnp.float32
    )
    bias_grad = jnp.concatenate(
        [
            jnp.sum(query_grad.reshape(row_count, model_width), axis=0),
            jnp.sum(value_grad.reshape(row_count, model_width), axis=0),
        ]
    )
    packed_grad = (
        jnp.stack([query_grad, key_grad, value_grad], axis=2)
        .reshape(row_count, 3 * model_width)
        .astype(jnp.bfloat16)
    )
    qkv_grad = contract_rows(attn_in, packed_grad)
    normed_one_grad = contract_cols(packed_grad, qkv_back)
    first_gain_grad = jnp.sum(normed_one_grad * normed_one, axis=0)
    first_shift_grad = jnp.sum(normed_one_grad, axis=0)
    input_grad = residual_grad + norm_back(normed_one_grad, normed_one, inv_one, gain_back_one)
    block_parts = (
        lax.psum_scatter(
            first_gain_grad.astype(jnp.bfloat16), "shard", scatter_dimension=0, tiled=True
        ).astype(jnp.float32),
        lax.psum_scatter(
            first_shift_grad.astype(jnp.bfloat16), "shard", scatter_dimension=0, tiled=True
        ).astype(jnp.float32),
        lax.psum_scatter(
            qkv_grad.astype(jnp.bfloat16), "shard", scatter_dimension=0, tiled=True
        ).astype(jnp.float32),
        lax.psum_scatter(
            bias_grad.astype(jnp.bfloat16), "shard", scatter_dimension=0, tiled=True
        ).astype(jnp.float32),
        lax.psum_scatter(
            proj_grad.astype(jnp.bfloat16), "shard", scatter_dimension=0, tiled=True
        ).astype(jnp.float32),
        lax.psum_scatter(
            proj_bias_grad.astype(jnp.bfloat16), "shard", scatter_dimension=0, tiled=True
        ).astype(jnp.float32),
        lax.psum_scatter(
            second_gain_grad.astype(jnp.bfloat16), "shard", scatter_dimension=0, tiled=True
        ).astype(jnp.float32),
        lax.psum_scatter(
            second_shift_grad.astype(jnp.bfloat16), "shard", scatter_dimension=0, tiled=True
        ).astype(jnp.float32),
        lax.psum_scatter(
            router_grad.astype(jnp.bfloat16), "shard", scatter_dimension=0, tiled=True
        ).astype(jnp.float32),
    )
    (
        gain_one_sum,
        shift_one_sum,
        qkv_sum,
        bias_sum,
        proj_sum,
        proj_bias_sum,
        gain_two_sum,
        shift_two_sum,
        router_sum,
    ) = (
        lax.psum(block_parts[0].astype(jnp.bfloat16), "expert").astype(jnp.float32),
        lax.psum(block_parts[1].astype(jnp.bfloat16), "expert").astype(jnp.float32),
        lax.psum(block_parts[2].astype(jnp.bfloat16), "expert").astype(jnp.float32),
        lax.psum(block_parts[3].astype(jnp.bfloat16), "expert").astype(jnp.float32),
        lax.psum(block_parts[4].astype(jnp.bfloat16), "expert").astype(jnp.float32),
        lax.psum(block_parts[5].astype(jnp.bfloat16), "expert").astype(jnp.float32),
        lax.psum(block_parts[6].astype(jnp.bfloat16), "expert").astype(jnp.float32),
        lax.psum(block_parts[7].astype(jnp.bfloat16), "expert").astype(jnp.float32),
        lax.psum(block_parts[8].astype(jnp.bfloat16), "expert").astype(jnp.float32),
    )
    return (
        block_output.reshape(image_count, seq_length, model_width),
        input_grad.reshape(image_count, seq_length, model_width),
        gain_one_sum,
        shift_one_sum,
        qkv_sum,
        bias_sum,
        proj_sum,
        proj_bias_sum,
        gain_two_sum,
        shift_two_sum,
        router_sum,
        in_weight_part,
        in_bias_part,
        out_weight_part,
        out_bias_part,
    )


def solution(mesh):
    in_specs = (
        P(("expert", "shard"), None, None),
        P(("expert", "shard")),
        P(("expert", "shard"), None, None),
        P("shard"),
        P("shard"),
        P("shard", None),
        P("shard"),
        P("shard", None),
        P("shard"),
        P("shard"),
        P("shard"),
        P("shard", None),
        P("expert", None, "shard"),
        P("expert", "shard"),
        P("expert", None, "shard"),
        P("expert", "shard"),
        P(("expert", "shard"), None, None),
    )
    out_specs = (
        P(("expert", "shard"), None, None),
        P(("expert", "shard"), None, None),
        P("shard"),
        P("shard"),
        P("shard", None),
        P("shard"),
        P("shard", None),
        P("shard"),
        P("shard"),
        P("shard"),
        P("shard", None),
        P("expert", None, "shard"),
        P("expert", "shard"),
        P("expert", None, "shard"),
        P("expert", "shard"),
    )
    return jax.shard_map(body, mesh=mesh, in_specs=in_specs, out_specs=out_specs, check_vma=False)
```

profile of v0, /device:TPU:0, one launch (start us, length us, event | category | flops | bytes accessed | tf_op | source)
XLA Modules:
  0.0 751.1 jit_solution(975591416569326734)
XLA Ops:
  13.9 22.0 %all-reduce.16 = (bf16[768]{0:T(1024)(128)(2,1)S(1)}, bf16[768]{0:T(1024)(128)(2,1)S(1)}, bf16[768]{0:T(1024)(128)(2,1)S(1)}, bf16[768]{0:T(1024)(128)(2,1)S(1)}...) all-reduce(bf16[768]{0:T(1024)(128)(2,1)S(1)} %dynamic-update-slice, ...), channel_id=1, replica_groups=mesh['expert'=8,'shard'=4] {'shard'}, use_global_device_ids=true, to_apply=%add.2 | all-reduce | flops 4608 | bytes 18432
  37.1 12.4 %all-gather = bf16[4,1,384]{2,1,0:T(2,128)(2,1)S(1)} all-gather(bf16[1,1,384]{2,1,0:T(2,128)(2,1)S(1)} %reshape.365), channel_id=1, replica_groups=mesh['expert'=8,'shard'=4] {'shard'}, dimensions={0}, use_global_device_ids=true | all-gather | bytes 3840 | tf_op jit(solution)/shard_map/all_gather | solution.py:141
  50.0 13.7 %all-gather.1 = bf16[4,192,8]{1,2,0:T(8,128)(2,1)S(1)} all-gather(bf16[1,192,8]{1,2,0:T(8,128)(2,1)S(1)} %bitcast.131), channel_id=1, replica_groups=mesh['expert'=8,'shard'=4] {'shard'}, dimensions={0}, use_global_device_ids=true | all-gather | bytes 15360 | tf_op jit(solution)/shard_map/all_gather | solution.py:146
  69.7 13.3 %all-gather.7.cloned.1.call-done = bf16[768,2304]{1,0:T(8,128)(2,1)} async-done(((bf16[192,2304]{1,0:T(8,128)(2,1)}), bf16[768,2304]{1,0:T(8,128)(2,1)}) %all-gather.7.cloned.1.call-update) | async-done | bytes 3538960 | tf_op jit(solution)/shard_map/all_gather | solution.py:140
  92.3 21.3 %all-gather.9.cloned.1.call-done = bf16[768,768]{1,0:T(8,128)(2,1)} async-done(((bf16[192,768]{1,0:T(8,128)(2,1)}), bf16[768,768]{1,0:T(8,128)(2,1)}) %all-gather.9.cloned.1.call-update) | async-done | bytes 1179664 | tf_op jit(solution)/shard_map/all_gather | solution.py:142
  120.3 3.9 all-to-all-start.2
  126.8 8.8 %all-to-all-done.2 = bf16[8,49,768]{2,1,0:T(8,128)(2,1)S(1)} async-done(((bf16[8,49,768]{2,1,0:T(8,128)(2,1)}), bf16[8,49,768]{2,1,0:T(8,128)(2,1)S(1)}, u32[]{:S(2)}, u32[]{:S(2)}) %all-to-all-start.2) | async-done | bytes 602144 | tf_op jit(solution)/shard_map/all_to_all | solution.py:238
  135.6 3.6 all-to-all-start
  139.2 14.6 %all_gather.56 = bf16[1,3072]{1,0:T(2,128)(2,1)S(1)} all-gather(bf16[1,768]{1,0:T(2,128)(2,1)S(1)} %copy-done.60), channel_id=1, replica_groups=mesh['expert'=8,'shard'=4] {'shard'}, dimensions={1}, use_global_device_ids=true | all-gather | bytes 7680 | tf_op jit(solution)/shard_map/all_gather | solution.py:150
  155.1 48.8 %all-gather.11.cloned.1.call-done = bf16[1,768,3072]{2,1,0:T(8,128)(2,1)} async-done(((bf16[1,768,768]{2,1,0:T(8,128)(2,1)}), bf16[1,768,3072]{2,1,0:T(8,128)(2,1)}) %all-gather.11.cloned.1.call-update) | async-done | bytes 4718608 | tf_op jit(solution)/shard_map/all_gather | solution.py:149
  203.9 6.9 multiply_convert_fusion
  210.9 82.4 %all-gather.13.cloned.1.call-done = bf16[1,3072,768]{1,2,0:T(8,128)(2,1)} async-done(((bf16[1,3072,192]{1,2,0:T(8,128)(2,1)}), bf16[1,3072,768]{1,2,0:T(8,128)(2,1)}) %all-gather.13.cloned.1.call-update) | async-done | bytes 4718608 | tf_op jit(solution)/shard_map/all_gather | solution.py:151
  293.2 6.4 fusion.96
  304.2 3.7 all-to-all-start.3
  307.9 5.1 fusion.24
  314.1 5.2 all-to-all-done.3
  319.4 4.2 all-to-all-start.1
  326.9 8.1 %all-to-all-done.1 = bf16[8,49,768]{2,1,0:T(8,128)(2,1)} async-done(((bf16[8,49,768]{2,1,0:T(8,128)(2,1)}), bf16[8,49,768]{2,1,0:T(8,128)(2,1)}, u32[]{:S(2)}, u32[]{:S(2)}) %all-to-all-start.1) | async-done | bytes 602144 | tf_op jit(solution)/shard_map/all_to_all | solution.py:216
  353.9 3.4 bitcast_reduce_fusion.1
  371.7 67.3 %reduce-scatter.16.cloned.1.call-done = bf16[192,2304]{1,0:T(8,128)(2,1)} async-done(((bf16[768,2304]{1,0:T(8,128)(2,1)}), bf16[192,2304]{1,0:T(8,128)(2,1)}) %reduce-scatter.16.cloned.1.call-update) | async-done | bytes 884752 | tf_op jit(solution)/shard_map/reduce_scatter | solution.py:345
  439.1 4.3 fusion.14
  443.4 20.3 %copy.168 = bf16[1,3072,768]{1,0,2:T(2,128)(2,1)} copy(bf16[1,3072,768]{2,1,0:T(8,128)(2,1)} %fusion.14) | data formatting | bytes 9437184
  463.8 7.5 %copy.181 = bf16[768,1,3072]{2,0,1:T(8,128)(2,1)} copy(bf16[768,1,3072]{2,1,0:T(2,128)(2,1)} %bitcast.122) | data formatting | bytes 9437184
  473.2 4.3 fusion.13
  481.9 4.0 reduce-scatter.24.cloned.1.call-done
  491.6 3.9 multiply_reduce_fusion.4
  495.4 18.1 %all-reduce.15 = (bf16[768]{0:T(1024)(128)(2,1)S(1)}, bf16[768]{0:T(1024)(128)(2,1)S(1)}, bf16[1536]{0:T(1024)(128)(2,1)S(1)}, bf16[768]{0:T(1024)(128)(2,1)S(1)...) all-reduce(bf16[768]{0:T(1024)(128)(2,1)} %get-tuple-element.92, ...), channel_id=2, replica_groups=mesh['expert'=8,'shard'=4] {'shard'}, use_global_device_ids=true, to_apply=%region_24.25.clone | all-reduce | flops 5376 | bytes 21504
  519.7 12.1 %all-reduce.13 = (bf16[192]{0:T(256)(128)(2,1)S(1)}, bf16[192]{0:T(256)(128)(2,1)S(1)}, bf16[384]{0:T(512)(128)(2,1)S(1)}, bf16[192]{0:T(256)(128)(2,1)S(1)}, bf...) all-reduce(bf16[192]{0:T(256)(128)(2,1)S(1)} %dynamic-slice.7, ...), channel_id=1, replica_groups=mesh['expert'=8,'shard'=4] {'expert'}, use_global_device_ids=true, to_apply=%region_25.26 | all-reduce | flops 2880 | bytes 11520 | tf_op jit(solution)/shard_map/psum | solution.py:378
  535.8 30.3 %all-reduce.19.cloned.1.call-done = (bf16[192,2304]{1,0:T(8,128)(2,1)}, bf16[192,768]{1,0:T(8,128)(2,1)}) async-done(((bf16[192,2304]{1,0:T(8,128)(2,1)}, bf16[192,768]{1,0:T(8,128)(2,1)}), (bf16[192,2304]{1,0:T(8,128)(2,1)}, bf16[192,768]{1,0:T(8,128)(2,1)})) %all-reduce.19.cloned.1.call-update) | async-done | bytes 1179664 | tf_op jit(solution)/shard_map/psum | solution.py:380
  570.4 82.6 %reduce-scatter.26.cloned.1.call-done = bf16[192,3072]{1,0:T(8,128)(2,1)} async-done(((bf16[768,3072]{1,0:T(8,128)(2,1)}), bf16[192,3072]{1,0:T(8,128)(2,1)}) %reduce-scatter.26.cloned.1.call-update) | async-done | bytes 1179664
  655.4 3.9 copy.169
  662.3 78.7 %reduce-scatter.20.cloned.1.call-done = bf16[1,768,768]{2,1,0:T(8,128)(2,1)} async-done(((bf16[1,768,3072]{2,1,0:T(8,128)(2,1)}), bf16[1,768,768]{2,1,0:T(8,128)(2,1)}) %reduce-scatter.20.cloned.1.call-update) | async-done | bytes 1179664 | tf_op jit(solution)/shard_map/reduce_scatter | solution.py:269
  (343 shorter events, 107.8 us)
Async XLA Ops:
  7.3 42.7 %copy-start.59 = (bf16[192,8]{0,1:T(8,128)(2,1)S(1)}, bf16[192,8]{0,1:T(8,128)(2,1)}, u32[]{:S(2)}) copy-start(bf16[192,8]{0,1:T(8,128)(2,1)} %param.28) | copy-start | bytes 9220
  7.3 59.0 %copy-start.24 = (f32[2,65,768]{2,0,1:T(2,128)S(1)}, f32[2,65,768]{2,0,1:T(2,128)}, u32[]{:S(2)}) copy-start(f32[2,65,768]{2,0,1:T(2,128)} %param.33) | copy-start | bytes 1198084
  7.3 75.7 %all-gather.7.cloned.1.call-start = ((), (), s32[]{:S(2)}) async-start(), calls=%async_computation.11 | async-start | bytes 4423680 | tf_op jit(solution)/shard_map/all_gather | solution.py:140
  8.1 105.5 %all-gather.9.cloned.1.call-start = ((), (), s32[]{:S(2)}) async-start(), calls=%async_computation.12 | async-start | bytes 1474560 | tf_op jit(solution)/shard_map/all_gather | solution.py:142
  8.8 195.1 %all-gather.11.cloned.1.call-start = ((), (), s32[]{:S(2)}) async-start(), calls=%async_computation.13 | async-start | bytes 5898240 | tf_op jit(solution)/shard_map/all_gather | solution.py:149
  9.5 283.7 %all-gather.13.cloned.1.call-start = ((), (), s32[]{:S(2)}) async-start(), calls=%async_computation.14 | async-start | bytes 5898240 | tf_op jit(solution)/shard_map/all_gather | solution.py:151
  11.1 38.8 %copy-start.48 = (s32[130]{0:T(256)}, s32[130]{0:T(256)S(1)}, u32[]{:S(2)}) copy-start(s32[130]{0:T(256)S(1)} %reshape.329) | copy-start | bytes 1564
  11.1 58.0 %copy-start.47 = (f32[130]{0:T(256)}, f32[130]{0:T(256)S(1)}, u32[]{:S(2)}) copy-start(f32[130]{0:T(256)S(1)} %convert_element_type.250) | copy-start | bytes 1564
  11.2 55.1 %copy-start.35 = (s32[130,2]{0,1:T(2,128)}, s32[130,2]{0,1:T(2,128)S(1)}, u32[]{:S(2)}) copy-start(s32[130,2]{0,1:T(2,128)S(1)} %eq.69) | copy-start | bytes 3124
  35.9 47.1 %copy-start.34 = (f32[768]{0:T(1024)}, f32[768]{0:T(1024)S(1)}, u32[]{:S(2)}) copy-start(f32[768]{0:T(1024)S(1)} %convert_element_type.241) | copy-start | bytes 9220
  35.9 79.6 %copy-start.33 = (f32[768]{0:T(1024)}, f32[768]{0:T(1024)S(1)}, u32[]{:S(2)}) copy-start(f32[768]{0:T(1024)S(1)} %convert_element_type.251) | copy-start | bytes 9220
  63.8 51.9 %copy-start.32 = (bf16[768,8]{0,1:T(8,128)(2,1)}, bf16[768,8]{0,1:T(8,128)(2,1)S(1)}, u32[]{:S(2)}) copy-start(bf16[768,8]{0,1:T(8,128)(2,1)S(1)} %reshape.368) | copy-start | bytes 36868
  66.5 47.1 %copy-start.1 = (f32[130,768]{1,0:T(8,128)}, f32[130,768]{1,0:T(8,128)S(1)}, u32[]{:S(2)}) copy-start(f32[130,768]{1,0:T(8,128)S(1)} %reshape.326) | copy-start | bytes 1198084
  91.1 26.9 %copy-start.12 = (f32[260,768]{1,0:T(8,128)S(1)}, f32[260,768]{1,0:T(8,128)}, u32[]{:S(2)}) copy-start(f32[260,768]{1,0:T(8,128)} %mul.291) | copy-start | bytes 2396164
  92.3 31.9 %copy-start.49 = (s32[130]{0:T(256)S(1)}, s32[130]{0:T(256)}, u32[]{:S(2)}) copy-start(s32[130]{0:T(256)} %copy-done.48) | copy-start | bytes 1564
  92.3 31.9 %copy-start.27 = (s32[130,2]{1,0:T(8,128)S(1)}, s32[130,2]{1,0:T(8,128)}, u32[]{:S(2)}) copy-start(s32[130,2]{1,0:T(8,128)} %copy.145) | copy-start | bytes 3124
  120.3 15.3 %all-to-all-start.2 = ((bf16[8,49,768]{2,1,0:T(8,128)(2,1)}), bf16[8,49,768]{2,1,0:T(8,128)(2,1)S(1)}, u32[]{:S(2)}, u32[]{:S(2)}) async-start(bf16[8,49,768]{2,1,0:T(8,128)(2,1)} %reshape.339), calls=%async_computation.2 | async-start | bytes 1376256 | tf_op jit(solution)/shard_map/all_to_all | solution.py:238
  135.6 19.3 %all-to-all-start = ((bf16[8,49,768]{2,1,0:T(8,128)(2,1)}), bf16[8,49,768]{2,1,0:T(8,128)(2,1)S(1)}, u32[]{:S(2)}, u32[]{:S(2)}) async-start(bf16[8,49,768]{2,1,0:T(8,128)(2,1)} %reshape.333), calls=%async_computation | async-start | bytes 1376256 | tf_op jit(solution)/shard_map/all_to_all | solution.py:205
  155.1 55.8 %copy-start.20 = (bf16[392,768]{1,0:T(8,128)(2,1)}, bf16[392,768]{1,0:T(8,128)(2,1)S(1)}, u32[]{:S(2)}) copy-start(bf16[392,768]{1,0:T(8,128)(2,1)S(1)} %reshape.334) | copy-start | bytes 1806340
  203.9 89.3 %copy-start.22 = (bf16[392,768]{1,0:T(8,128)(2,1)S(1)}, bf16[392,768]{1,0:T(8,128)(2,1)}, u32[]{:S(2)}) copy-start(bf16[392,768]{1,0:T(8,128)(2,1)} %reshape.340) | copy-start | bytes 1806340
  304.2 15.1 %all-to-all-start.3 = ((bf16[8,49,768]{2,1,0:T(8,128)(2,1)}), bf16[8,49,768]{2,1,0:T(8,128)(2,1)S(1)}, u32[]{:S(2)}, u32[]{:S(2)}) async-start(bf16[8,49,768]{2,1,0:T(8,128)(2,1)} %reshape.341), calls=%async_computation.3 | async-start | bytes 1376256 | tf_op jit(solution)/shard_map/all_to_all | solution.py:260
  319.4 15.7 %all-to-all-start.1 = ((bf16[8,49,768]{2,1,0:T(8,128)(2,1)}), bf16[8,49,768]{2,1,0:T(8,128)(2,1)}, u32[]{:S(2)}, u32[]{:S(2)}) async-start(bf16[8,49,768]{2,1,0:T(8,128)(2,1)} %reshape.335), calls=%async_computation.1 | async-start | bytes 1376256 | tf_op jit(solution)/shard_map/all_to_all | solution.py:216
  323.6 48.2 %reduce-scatter.18.cloned.1.call-start = ((), (), s32[]{:S(2)}) async-start(), calls=%async_computation.16 | async-start | bytes 1474560 | tf_op jit(solution)/shard_map/reduce_scatter | solution.py:351
  345.6 93.4 %reduce-scatter.16.cloned.1.call-start = ((), (), s32[]{:S(2)}) async-start(), calls=%async_computation.15 | async-start | bytes 4423680 | tf_op jit(solution)/shard_map/reduce_scatter | solution.py:345
  367.1 72.0 %copy-start.23 = (bf16[392,768]{1,0:T(8,128)(2,1)S(1)}, bf16[392,768]{1,0:T(8,128)(2,1)}, u32[]{:S(2)}) copy-start(bf16[392,768]{1,0:T(8,128)(2,1)} %reshape.340) | copy-start | bytes 1806340
  367.1 112.1 %reduce-scatter.28.cloned.1.call-start = ((), (), s32[]{:S(2)}) async-start(), calls=%async_computation.21 | async-start | bytes 245760
  367.3 71.8 %copy-start.74 = (bf16[392,3072]{1,0:T(8,128)(2,1)S(1)}, bf16[392,3072]{1,0:T(8,128)(2,1)}, u32[]{:S(2)}) copy-start(bf16[392,3072]{1,0:T(8,128)(2,1)} %get-tuple-element.137) | copy-start | bytes 7225348
  368.2 117.8 %reduce-scatter.24.cloned.1.call-start = ((), (), s32[]{:S(2)}) async-start(), calls=%async_computation.19 | async-start | bytes 983040
  369.6 149.2 %reduce-scatter.22.cloned.1.call-start = ((), (), s32[]{:S(2)}) async-start(), calls=%async_computation.18 | async-start | bytes 245760
  370.7 195.4 %all-reduce.19.cloned.1.call-start = ((), (), s32[]{:S(2)}) async-start(), calls=%async_computation.22 | async-start | bytes 2359296 | tf_op jit(solution)/shard_map/psum | solution.py:380
  439.0 213.9 %reduce-scatter.26.cloned.1.call-start = ((), (), s32[]{:S(2)}) async-start(), calls=%async_computation.20 | async-start | bytes 5898240
  471.3 269.6 %reduce-scatter.20.cloned.1.call-start = ((), (), s32[]{:S(2)}) async-start(), calls=%async_computation.17 | async-start | bytes 5898240 | tf_op jit(solution)/shard_map/reduce_scatter | solution.py:269
  (61 other events, 658.2 us)
Sparse Core Ops, SparseCore 0:
  9.7 73.3 all-gather.6
  84.6 28.8 all-gather.8
  115.1 88.7 all-gather.10
  205.4 87.8 all-gather.12
  345.8 25.9 reduce-scatter.17
  373.9 65.0 reduce-scatter.15
  441.8 19.7 reduce-scatter.27
  464.5 21.3 reduce-scatter.23
  488.2 19.1 reduce-scatter.21
  510.4 55.6 all-reduce.18
  568.4 84.5 reduce-scatter.25
  655.1 85.7 reduce-scatter.19
where the time goes:
time: 761 us; the launch traced here: 751 us
  waiting for transfers between devices  454 us (60%)
  blocking collectives  93 us (12%)
  local copies, waits for them, and re-layouts  78.9 us (10%)
  matrix products  60.7 us (8%)
  other arithmetic  29.7 us (4%)
  between operations  18.1 us (2%)
  starting transfers between devices  16.2 us (2%)
    unnamed x16, waiting for transfers between devices  89.3 us
    all_gather x1, waiting for transfers between devices, body(): lax.all_gather(expert_out_weight, 'shard', axis=2, tiled=True)  82.4 us
    reduce_scatter x1, waiting for transfers between devices, body(): lax.psum_scatter(in_weight_grad[None].astype(jnp.bfloat16), 'shard', scat...  78.7 us
    reduce_scatter x1, waiting for transfers between devices, body(): lax.psum_scatter(qkv_grad.astype(jnp.bfloat16), 'shard', scatter_dimensio...  67.3 us
    unnamed x197, local copies, waits for them, and re-layouts  57.3 us
    all_gather x1, waiting for transfers between devices, body(): lax.all_gather(expert_in_weight, 'shard', axis=2, tiled=True)  48.8 us
    unnamed x2, blocking collectives  40.1 us
    psum x1, waiting for transfers between devices, body(): lax.psum(block_parts[2].astype(jnp.bfloat16), 'expert').astype(jnp.float32)  30.3 us
  transfers between devices with their start and end apart: 16, of which 13 were waited for; matrix products, arithmetic and copies ran while one was open for 19% of the time, Pallas kernels for 0%

commit v1 on v0

v1 whole, which is shorter than its diff:
```python
import math

import jax
import jax.numpy as jnp
from jax import lax
from jax.sharding import PartitionSpec as P

HEADS = 12
HEAD_DIM = 64


EPSILON = 1e-06
PRECISE = lax.Precision.HIGHEST
HALF_ROOT = 0.7071067811865476
DENSITY = 0.3989422804014327


def as_float(array_in):
    return array_in.astype(jnp.float32)


def contract_rows(left_side, right_side):
    return lax.dot_general(
        left_side, right_side, (((0,), (0,)), ((), ())), preferred_element_type=jnp.float32
    )


def contract_cols(left_side, right_side):
    return lax.dot_general(
        left_side, right_side, (((1,), (1,)), ((), ())), preferred_element_type=jnp.float32
    )


def precise_rows(left_side, right_side):
    return lax.dot_general(
        left_side,
        right_side,
        (((0,), (0,)), ((), ())),
        precision=PRECISE,
        preferred_element_type=jnp.float32,
    )


def precise_cols(left_side, right_side):
    return lax.dot_general(
        left_side,
        right_side,
        (((1,), (1,)), ((), ())),
        precision=PRECISE,
        preferred_element_type=jnp.float32,
    )


def layer_norm(values_in, gain_vec, shift_vec):
    center = values_in - jnp.mean(values_in, axis=-1, keepdims=True)
    inv_std = lax.rsqrt(jnp.mean(center * center, axis=-1, keepdims=True) + EPSILON)
    normed = center * inv_std
    return (normed * as_float(gain_vec) + as_float(shift_vec), normed, inv_std)


def norm_back(upstream, normed, inv_std, gain_vec):
    scaled = upstream * as_float(gain_vec)
    return inv_std * (
        scaled
        - jnp.mean(scaled, axis=-1, keepdims=True)
        - normed * jnp.mean(scaled * normed, axis=-1, keepdims=True)
    )


def gelu_parts(pre_act):
    normal_cdf = 0.5 * (1.0 + jax.scipy.special.erf(pre_act * HALF_ROOT))
    return (
        pre_act * normal_cdf,
        normal_cdf + pre_act * DENSITY * jnp.exp(-0.5 * pre_act * pre_act),
    )


def slot_places(expert_routes, image_live, expert_count):
    row_count = expert_routes.shape[0] * expert_routes.shape[1]
    flat_routes = expert_routes.reshape(2 * row_count)
    live_rows = jnp.repeat(image_live, expert_routes.shape[1])
    alive_pairs = jnp.repeat(live_rows, 2)
    chosen = (flat_routes[:, None] == jnp.arange(expert_count, dtype=jnp.int32)[None, :]).astype(
        jnp.int32
    )
    live_hits = chosen * alive_pairs[:, None]
    earlier = (
        jnp.arange(2 * row_count, dtype=jnp.int32)[:, None]
        > jnp.arange(2 * row_count, dtype=jnp.int32)[None, :]
    ).astype(jnp.bfloat16)
    counted = jnp.dot(earlier, live_hits.astype(jnp.bfloat16), preferred_element_type=jnp.float32)
    position = jnp.sum(counted * as_float(live_hits), axis=1)
    route_code = jnp.where(alive_pairs > 0, flat_routes, -1).astype(jnp.float32)
    return (
        chosen.reshape(row_count, 2, expert_count),
        route_code.reshape(row_count, 2),
        position.reshape(row_count, 2),
        live_rows,
    )


def attention_scores(query_rows, key_rows):
    return jnp.einsum(
        "bqhd,bkhd->bhqk", query_rows, key_rows, preferred_element_type=jnp.float32
    ) * (1.0 / math.sqrt(HEAD_DIM))


def gather_all(piece):
    return lax.all_gather(piece, ("shard", "expert"), axis=0, tiled=True)


def body(
    block_input,
    image_live,
    expert_routes,
    first_gain,
    first_shift,
    qkv_weight,
    query_value_bias,
    attn_out_weight,
    attn_out_bias,
    second_gain,
    second_shift,
    router_weight,
    expert_in_weight,
    expert_in_bias,
    expert_out_weight,
    expert_out_bias,
    output_grad,
):
    image_count, seq_length, width = block_input.shape
    row_count = image_count * seq_length
    shards = lax.axis_size("shard")
    experts = lax.axis_size("expert")
    expert_count = router_weight.shape[1]
    my_shard = lax.axis_index("shard")
    my_expert = lax.axis_index("expert")
    shard_rows = first_gain.shape[0]
    piece_rows = shard_rows // experts
    capacity = (3 * row_count + expert_count - 1) // expert_count
    group_rows = -(-shards * capacity // 16) * 16
    slot_rows = expert_count * group_rows
    sent_rows = -(-row_count // 16) * 16
    spare_rows = sent_rows - row_count
    bf16 = jnp.bfloat16

    vectors = jnp.stack(
        [
            first_gain,
            first_shift,
            attn_out_bias,
            second_gain,
            second_shift,
            query_value_bias[:shard_rows],
            query_value_bias[shard_rows:],
        ],
        axis=1,
    )
    extra = jnp.concatenate([vectors, router_weight], axis=1)
    vector_count = vectors.shape[1]
    extra = jnp.pad(extra, ((0, 0), (0, 128 - extra.shape[1])))
    packed_params = jnp.concatenate([qkv_weight, extra], axis=1)
    piece = lax.dynamic_slice_in_dim(packed_params, my_expert * piece_rows, piece_rows, axis=0)
    proj_piece = lax.dynamic_slice_in_dim(
        attn_out_weight, my_expert * piece_rows, piece_rows, axis=0
    )
    whole = gather_all(piece)
    proj_piece, whole = lax.optimization_barrier((proj_piece, whole))
    proj_full = gather_all(proj_piece)
    qkv_full = whole[:, : 3 * width]
    extra_t = as_float(whole[:, 3 * width :].T)
    gain_one, shift_one, proj_bias, gain_two, shift_two = (extra_t[i] for i in range(5))
    bias_full = jnp.stack(
        [extra_t[5].reshape(shards, shard_rows), extra_t[6].reshape(shards, shard_rows)], axis=1
    ).reshape(2 * width)
    router_t = extra_t[vector_count : vector_count + expert_count].astype(bf16)

    out_slice = lax.all_to_all(
        expert_out_weight[0], "shard", split_axis=0, concat_axis=1, tiled=True
    )
    in_slice = expert_in_weight[0]

    chosen, route_code, position, live_rows = slot_places(expert_routes, image_live, expert_count)
    live_col = as_float(live_rows)[:, None]
    upstream = output_grad.reshape(row_count, width) * live_col
    sent_up = jnp.pad(upstream.astype(bf16), ((0, spare_rows), (0, 0)))
    sent_up, proj_full = lax.optimization_barrier((sent_up, proj_full))
    line_up = lax.all_gather(sent_up, "shard", axis=0, tiled=True)

    flat_tokens = block_input.reshape(row_count, width)
    norm_out, normed_one, inv_one = layer_norm(flat_tokens, gain_one, shift_one)
    attn_in = norm_out.astype(bf16)
    bias_row = jnp.concatenate(
        [bias_full[:width], jnp.zeros((width,), jnp.float32), bias_full[width:]]
    )
    packed = (
        (jnp.dot(attn_in, qkv_full, preferred_element_type=jnp.float32) + bias_row)
        .astype(bf16)
        .reshape(image_count, seq_length, 3, HEADS, HEAD_DIM)
    )
    query_rows = packed[:, :, 0]
    key_rows = packed[:, :, 1]
    value_rows = packed[:, :, 2]
    scores = attention_scores(query_rows, key_rows)
    row_max = jnp.max(scores, axis=-1, keepdims=True)
    log_total = row_max + jnp.log(jnp.sum(jnp.exp(scores - row_max), axis=-1, keepdims=True))
    probs = jnp.exp(scores - log_total)
    weights = probs.astype(bf16)
    mixed_heads = (
        jnp.einsum("bhqk,bkhd->bqhd", weights, value_rows, preferred_element_type=jnp.float32)
        .astype(bf16)
        .reshape(row_count, width)
    )
    residual = (
        flat_tokens
        + jnp.dot(mixed_heads, proj_full, preferred_element_type=jnp.float32)
        + proj_bias
    )
    norm_two_out, normed_two, inv_two = layer_norm(residual, gain_two, shift_two)
    expert_in = norm_two_out.astype(bf16)
    logits = contract_cols(expert_in, router_t)
    shifted = jnp.exp(logits - jnp.max(logits, axis=-1, keepdims=True))
    gate_probs = shifted / jnp.sum(shifted, axis=-1, keepdims=True)
    gate_pick = jnp.sum(gate_probs[:, None, :] * as_float(chosen), axis=2)

    gate_high = gate_pick.astype(bf16)
    gate_low = (gate_pick - as_float(gate_high)).astype(bf16)
    notes = jnp.concatenate(
        [gate_high, gate_low, route_code.astype(bf16), position.astype(bf16)], axis=1
    )
    notes = jnp.pad(notes, ((0, 0), (0, 128 - notes.shape[1])))
    sent_line = jnp.concatenate([expert_in, notes], axis=1)
    sent_line = jnp.pad(sent_line, ((0, spare_rows), (0, 0)))
    line = lax.all_gather(sent_line, "shard", axis=0, tiled=True)
    line_rows = shards * sent_rows
    line_in = line[:, :width]
    line_notes = as_float(line[:, width : width + 8])
    line_gate = line_notes[:, 0:2] + line_notes[:, 2:4]
    line_ids = jnp.arange(line_rows, dtype=jnp.int32)[:, None]
    owner = line_ids // sent_rows
    filled = line_ids % sent_rows < row_count
    line_slot = (
        line_notes[:, 4:6].astype(jnp.int32) * group_rows
        + owner * capacity
        + line_notes[:, 6:8].astype(jnp.int32)
    )
    line_slot = jnp.where(filled & (line_notes[:, 4:6] >= 0), line_slot, -1)
    slot_ids = jnp.arange(slot_rows, dtype=jnp.int32)
    table_0 = line_slot[:, 0:1] == slot_ids[None, :]
    table_1 = line_slot[:, 1:2] == slot_ids[None, :]
    send_table = (table_0 | table_1).astype(bf16)
    grad_table = (
        jnp.where(table_0, line_gate[:, 0:1], 0.0) + jnp.where(table_1, line_gate[:, 1:2], 0.0)
    ).astype(bf16)
    outgoing = contract_rows(send_table, line_in).astype(bf16)
    incoming = lax.all_to_all(outgoing, "expert", split_axis=0, concat_axis=0, tiled=True)
    grad_out = contract_rows(grad_table, line_up).astype(bf16)
    grad_in = lax.all_to_all(grad_out, "expert", split_axis=0, concat_axis=0, tiled=True)

    pre_act = jnp.dot(incoming, in_slice, preferred_element_type=jnp.float32) + as_float(
        expert_in_bias
    )
    gelu_out, gelu_slope = gelu_parts(pre_act)
    gelu_bf = gelu_out.astype(bf16)
    own_bias = lax.dynamic_update_slice(
        jnp.zeros((1, width), jnp.float32),
        as_float(expert_out_bias),
        (0, my_shard * shard_rows),
    )
    expert_out = (
        jnp.dot(gelu_bf, out_slice, preferred_element_type=jnp.float32) + own_bias
    ).astype(bf16)
    returned = lax.all_to_all(expert_out, "expert", split_axis=0, concat_axis=0, tiled=True)
    pre_grad = contract_cols(grad_in, out_slice) * gelu_slope
    in_bias_part = jnp.sum(pre_grad, axis=0)[None]
    pre_bf = pre_grad.astype(bf16)
    back_rows = contract_cols(pre_bf, in_slice).astype(bf16)
    returned_grad = lax.all_to_all(back_rows, "expert", split_axis=0, concat_axis=0, tiled=True)
    out_weight_grad = contract_rows(gelu_bf, grad_in).astype(bf16)
    out_weight_part = as_float(
        lax.all_to_all(out_weight_grad, "shard", split_axis=1, concat_axis=0, tiled=True)
    )[None]
    in_weight_part = contract_rows(incoming, pre_bf)[None]
    out_bias_part = lax.dynamic_slice_in_dim(
        jnp.sum(as_float(grad_in), axis=0), my_shard * shard_rows, shard_rows
    )[None]

    out_0 = jnp.dot(table_0.astype(bf16), returned, preferred_element_type=jnp.float32)
    out_1 = jnp.dot(table_1.astype(bf16), returned, preferred_element_type=jnp.float32)
    combined = line_gate[:, 0:1] * out_0 + line_gate[:, 1:2] * out_1
    line_up_wide = as_float(line_up)
    gate_grad_line = jnp.stack(
        [jnp.sum(line_up_wide * out_0, axis=1), jnp.sum(line_up_wide * out_1, axis=1)], axis=1
    )
    summed = as_float(
        lax.psum_scatter(
            jnp.concatenate(
                [
                    combined.astype(bf16),
                    jnp.pad(gate_grad_line, ((0, 0), (0, 126))).astype(bf16),
                ],
                axis=1,
            ),
            "shard",
            scatter_dimension=0,
            tiled=True,
        )
    )[:row_count]
    block_output = residual + summed[:, :width]
    gate_grad = summed[:, width : width + 2]
    back_line = jnp.dot(send_table, returned_grad, preferred_element_type=jnp.float32)
    route_grad = as_float(
        lax.psum_scatter(back_line.astype(bf16), "shard", scatter_dimension=0, tiled=True)
    )[:row_count]

    full_gate_grad = jnp.sum(gate_grad[:, :, None] * as_float(chosen), axis=1)
    logit_grad = gate_probs * (
        full_gate_grad - jnp.sum(gate_probs * full_gate_grad, axis=-1, keepdims=True)
    )
    router_grad_t = contract_rows(logit_grad, as_float(expert_in))
    normed_two_grad = route_grad + jnp.dot(
        logit_grad, as_float(router_t), preferred_element_type=jnp.float32
    )
    second_gain_grad = jnp.sum(normed_two_grad * normed_two, axis=0)
    second_shift_grad = jnp.sum(normed_two_grad, axis=0)
    residual_grad = upstream + norm_back(normed_two_grad, normed_two, inv_two, gain_two)
    proj_bias_grad = jnp.sum(residual_grad, axis=0)
    residual_bf = residual_grad.astype(bf16)
    proj_grad = contract_rows(mixed_heads, residual_bf)
    mixed_grad = (
        contract_cols(residual_bf, proj_full)
        .astype(bf16)
        .reshape(image_count, seq_length, HEADS, HEAD_DIM)
    )
    value_grad = jnp.einsum(
        "bhqk,bqhd->bkhd", weights, mixed_grad, preferred_element_type=jnp.float32
    )
    prob_grad = jnp.einsum(
        "bqhd,bkhd->bhqk", mixed_grad, value_rows, preferred_element_type=jnp.float32
    )
    score_grad = (
        probs
        * (prob_grad - jnp.sum(probs * prob_grad, axis=-1, keepdims=True))
        * (1.0 / math.sqrt(HEAD_DIM))
    ).astype(bf16)
    query_grad = jnp.einsum(
        "bhqk,bkhd->bqhd", score_grad, key_rows, preferred_element_type=jnp.float32
    )
    key_grad = jnp.einsum(
        "bhqk,bqhd->bkhd", score_grad, query_rows, preferred_element_type=jnp.float32
    )
    query_bias_grad = jnp.sum(query_grad.reshape(row_count, width), axis=0)
    value_bias_grad = jnp.sum(value_grad.reshape(row_count, width), axis=0)
    packed_grad = (
        jnp.stack([query_grad, key_grad, value_grad], axis=2)
        .reshape(row_count, 3 * width)
        .astype(bf16)
    )
    qkv_grad = contract_rows(attn_in, packed_grad)
    normed_one_grad = contract_cols(packed_grad, qkv_full)
    first_gain_grad = jnp.sum(normed_one_grad * normed_one, axis=0)
    first_shift_grad = jnp.sum(normed_one_grad, axis=0)
    input_grad = residual_grad + norm_back(normed_one_grad, normed_one, inv_one, gain_one)

    bias_grad = jnp.concatenate([query_bias_grad, value_bias_grad]).reshape(shards, 2, shard_rows)
    extra_grad = jnp.concatenate(
        [
            jnp.stack(
                [
                    first_gain_grad,
                    first_shift_grad,
                    proj_bias_grad,
                    second_gain_grad,
                    second_shift_grad,
                    bias_grad[:, 0].reshape(width),
                    bias_grad[:, 1].reshape(width),
                ]
            ),
            router_grad_t,
        ],
        axis=0,
    )
    extra_grad = jnp.pad(extra_grad, ((0, 128 - extra_grad.shape[0]), (0, 0)))
    grads = jnp.concatenate(
        [qkv_grad.astype(bf16), proj_grad.astype(bf16), extra_grad.astype(bf16).T], axis=1
    )
    mine = lax.psum_scatter(grads, ("shard", "expert"), scatter_dimension=0, tiled=True)
    sums = as_float(lax.all_gather(mine, "expert", axis=0, tiled=True))
    side_t = sums[:, 4 * width :].T
    return (
        block_output.reshape(image_count, seq_length, width),
        input_grad.reshape(image_count, seq_length, width),
        side_t[0],
        side_t[1],
        sums[:, : 3 * width],
        side_t[5:7].reshape(2 * shard_rows),
        sums[:, 3 * width : 4 * width],
        side_t[2],
        side_t[3],
        side_t[4],
        sums[:, 4 * width + vector_count : 4 * width + vector_count + expert_count],
        in_weight_part,
        in_bias_part,
        out_weight_part,
        out_bias_part,
    )


def solution(mesh):
    in_specs = (
        P(("expert", "shard"), None, None),
        P(("expert", "shard")),
        P(("expert", "shard"), None, None),
        P("shard"),
        P("shard"),
        P("shard", None),
        P("shard"),
        P("shard", None),
        P("shard"),
        P("shard"),
        P("shard"),
        P("shard", None),
        P("expert", None, "shard"),
        P("expert", "shard"),
        P("expert", None, "shard"),
        P("expert", "shard"),
        P(("expert", "shard"), None, None),
    )
    out_specs = (
        P(("expert", "shard"), None, None),
        P(("expert", "shard"), None, None),
        P("shard"),
        P("shard"),
        P("shard", None),
        P("shard"),
        P("shard", None),
        P("shard"),
        P("shard"),
        P("shard"),
        P("shard", None),
        P("expert", None, "shard"),
        P("expert", "shard"),
        P("expert", None, "shard"),
        P("expert", "shard"),
    )
    return jax.shard_map(body, mesh=mesh, in_specs=in_specs, out_specs=out_specs, check_vma=False)
```

time: 761 us -> 528 us (0.69)
  waiting for transfers between devices: 454 us -> 280 us
  blocking collectives: 93 us -> 42.2 us
  local copies, waits for them, and re-layouts: 78.9 us -> 53 us
  matrix products: 60.7 us -> 80.9 us
  starting transfers between devices: 16.2 us -> 28.7 us
  other arithmetic: 29.7 us -> 20 us
    reduce_scatter x3 -> x2, waiting for transfers between devices: 147 us -> 26 us  [the longest x1 24.9 us: body(): lax.psum_scatter(back_line.astype(bf16), 'shard', scatter_dimension=0, ti...]
    all_gather x4 -> x3, waiting for transfers between devices: 166 us -> 99.3 us  [the longest x2 90.7 us: gather_all(): return lax.all_gather(piece, ('shard', 'expert'), axis=0, tiled=True)]
    unnamed x197 -> x79, local copies, waits for them, and re-layouts: 57.3 us -> 14 us
    unnamed x2 -> x0, blocking collectives: 40.1 us -> none
    psum x1 -> x0, waiting for transfers between devices: 30.3 us -> none  [body(): lax.psum(block_parts[2].astype(jnp.bfloat16), 'expert').astype(jnp.float32)]
    all_to_all x2 -> x4, waiting for transfers between devices: 13.3 us -> 40 us  [the longest x1 20.5 us: body(): lax.all_to_all(back_rows, 'expert', split_axis=0, concat_axis=0, tiled=True)]
    convert_element_type x14 -> x5, other arithmetic: 14.8 us -> 0.62 us  [the longest x1 0.36 us: body(): attn_in = norm_out.astype(bf16)]
    psum x1 -> x0, blocking collectives: 12.1 us -> none  [body(): lax.psum(block_parts[0].astype(jnp.bfloat16), 'expert').astype(jnp.float32)]
  transfers between devices with their start and end apart: 16 -> 12, of which waited for: 13 -> 10; matrix products, arithmetic and copies ran while one was open for 19% -> 21% of each run, Pallas kernels for 0% -> 0%
where the time goes in v1:
time: 528 us; the launch traced here: 520 us
  waiting for transfers between devices  280 us (53%)
  matrix products  80.9 us (15%)
  local copies, waits for them, and re-layouts  53 us (10%)
  blocking collectives  42.2 us (8%)
  starting transfers between devices  28.7 us (5%)
  other arithmetic  20 us (4%)
  between operations  15.3 us (3%)
    all_gather x2, waiting for transfers between devices, gather_all(): return lax.all_gather(piece, ('shard', 'expert'), axis=0, tiled=True)  90.7 us
    unnamed x7, waiting for transfers between devices  90.4 us
    reduce_scatter x1, waiting for transfers between devices, body(): lax.psum_scatter(back_line.astype(bf16), 'shard', scatter_dimension=0, ti...  24.9 us
    dot_general x7, matrix products, contract_rows(): lax.dot_general(left_side, right_side, (((0,), (0,)), ((), ())), preferre...  22.8 us
    all_gather x1, blocking collectives, body(): line = lax.all_gather(sent_line, 'shard', axis=0, tiled=True)  22 us
    all_to_all x1, waiting for transfers between devices, body(): lax.all_to_all(back_rows, 'expert', split_axis=0, concat_axis=0, tiled=True)  20.5 us
    all_gather x1, blocking collectives, body(): line_up = lax.all_gather(sent_up, 'shard', axis=0, tiled=True)  20.2 us
    all_to_all x1, waiting for transfers between devices, body(): lax.all_to_all(expert_out, 'expert', split_axis=0, concat_axis=0, tiled=T...  19.5 us
  transfers between devices with their start and end apart: 12, of which 10 were waited for; matrix products, arithmetic and copies ran while one was open for 21% of the time, Pallas kernels for 0%

profile of v1, /device:TPU:0, one launch (start us, length us, event | category | flops | bytes accessed | tf_op | source)
XLA Modules:
  0.0 520.1 jit_solution(12388158914356415641)
XLA Ops:
  14.0 2.7 all_to_all.59
  17.9 6.5 %all-to-all-start.1 = ((bf16[4,768,192]{1,2,0:T(8,128)(2,1)}), bf16[4,768,192]{1,2,0:T(8,128)(2,1)}, u32[]{:S(2)}, u32[]{:S(2)}) async-start(bf16[4,768,192]{1,2,0:T(8,128)(2,1)} %copy.218), calls=%async_computation.1 | async-start | bytes 2359296 | tf_op jit(solution)/shard_map/all_to_all | solution.py:178
  31.3 58.2 %all-gather.4.cloned.1.call-done = bf16[768,2432]{1,0:T(8,128)(2,1)} async-done(((bf16[24,2432]{1,0:T(8,128)(2,1)}), bf16[768,2432]{1,0:T(8,128)(2,1)}) %all-gather.4.cloned.1.call-update) | async-done | bytes 3735568 | tf_op jit(solution)/shard_map/all_gather | solution.py:109
  93.1 3.6 fusion.8
  112.6 32.5 %all-gather.6.cloned.1.call-done = bf16[768,768]{1,0:T(8,128)(2,1)} async-done(((bf16[24,768]{1,0:T(8,128)(2,1)}), bf16[768,768]{1,0:T(8,128)(2,1)}) %all-gather.6.cloned.1.call-update) | async-done | bytes 1179664 | tf_op jit(solution)/shard_map/all_gather | solution.py:109
  148.8 22.0 %all_gather.17 = bf16[576,896]{1,0:T(8,128)(2,1)S(1)} all-gather(bf16[144,896]{1,0:T(8,128)(2,1)S(1)} %pad.29), channel_id=1, replica_groups=mesh['expert'=8,'shard'=4] {'shard'}, dimensions={0}, use_global_device_ids=true | all-gather | bytes 1290240 | tf_op jit(solution)/shard_map/all_gather | solution.py:234
  172.2 4.2 convolution_convert_fusion.2
  176.4 4.4 all-to-all-start
  181.2 20.2 %all_gather.18 = bf16[576,768]{1,0:T(8,128)(2,1)S(1)} all-gather(bf16[144,768]{1,0:T(8,128)(2,1)} %pad.27), channel_id=1, replica_groups=mesh['expert'=8,'shard'=4] {'shard'}, dimensions={0}, use_global_device_ids=true | all-gather | bytes 1105920 | tf_op jit(solution)/shard_map/all_gather | solution.py:188
  202.3 4.4 convolution_convert_fusion.3
  206.7 5.6 %all-to-all-done = bf16[8,208,768]{2,1,0:T(8,128)(2,1)} async-done(((bf16[8,208,768]{2,1,0:T(8,128)(2,1)}), bf16[8,208,768]{2,1,0:T(8,128)(2,1)}, u32[]{:S(2)}, u32[]{:S(2)}) %all-to-all-start) | async-done | bytes 2555936 | tf_op jit(solution)/shard_map/all_to_all | solution.py:256
  212.3 4.5 all-to-all-start.3
  217.2 6.0 %multiply_convert_fusion = (bf16[1664,768]{1,0:T(8,128)(2,1)S(1)}, f32[1664,768]{1,0:T(8,128)}) fusion(f32[768]{0:T(1024)S(1)} %convert_reduce_fusion.1, bf16[1664,768]{1,0:T(8,128)(2,1)} %bitcast.6, bf16[1,768,768]{2,1,0:T(8,128)(2,1)S(1)} %copy-done), kind=kOutput, calls=%fused_computation.8 | convolution fusion | flops 1970601984 | bytes 11406336 | tf_op jit(solution)/shard_map/dot_general | solution.py:260
  224.7 5.0 add_convert_fusion
  229.7 18.7 %all-to-all-done.3 = bf16[8,208,768]{2,1,0:T(8,128)(2,1)} async-done(((bf16[8,208,768]{2,1,0:T(8,128)(2,1)}), bf16[8,208,768]{2,1,0:T(8,128)(2,1)}, u32[]{:S(2)}, u32[]{:S(2)}) %all-to-all-start.3) | async-done | bytes 2555936 | tf_op jit(solution)/shard_map/all_to_all | solution.py:258
  248.4 4.6 all-to-all-start.2
  252.9 6.9 %fusion.111 = (f32[768]{0:T(1024)}, bf16[1664,768]{1,0:T(8,128)(2,1)S(1)}) fusion(f32[1664,768]{1,0:T(8,128)} %get-tuple-element.163, f32[768]{0:T(1024)S(1)} %convert_reduce_fusion.1, bf16[1664,768]{1,0:T(8,128)(2,1)} %bitcast.14, bf16[768,768]{0,1:T(8,128)(2,1)} %bitcast.9), kind=kOutput, calls=%fused_computation.215 | convolution fusion | flops 1978268928 | bytes 11409408 | tf_op jit(solution)/shard_map/dot_general | solution.py:29
  261.2 3.7 convolution_convert_fusion.1
  265.0 19.5 %all-to-all-done.2 = bf16[8,208,768]{2,1,0:T(8,128)(2,1)} async-done(((bf16[8,208,768]{2,1,0:T(8,128)(2,1)}), bf16[8,208,768]{2,1,0:T(8,128)(2,1)}, u32[]{:S(2)}, u32[]{:S(2)}) %all-to-all-start.2) | async-done | bytes 2555936 | tf_op jit(solution)/shard_map/all_to_all | solution.py:273
  284.5 4.4 all-to-all-start.4
  289.0 3.7 fusion.5
  292.7 4.8 fusion.27
  299.9 20.5 %all-to-all-done.4 = bf16[8,208,768]{2,1,0:T(8,128)(2,1)} async-done(((bf16[8,208,768]{2,1,0:T(8,128)(2,1)}), bf16[8,208,768]{2,1,0:T(8,128)(2,1)}, u32[]{:S(2)}, u32[]{:S(2)}) %all-to-all-start.4) | async-done | bytes 2555936 | tf_op jit(solution)/shard_map/all_to_all | solution.py:278
  320.4 4.8 fusion.29
  328.8 24.9 %reduce-scatter.8.cloned.1.call-done = bf16[144,768]{1,0:T(8,128)(2,1)} async-done(((bf16[576,768]{1,0:T(8,128)(2,1)}), bf16[144,768]{1,0:T(8,128)(2,1)}) %reduce-scatter.8.cloned.1.call-update) | async-done | bytes 221200 | tf_op jit(solution)/shard_map/reduce_scatter | solution.py:313
  369.7 2.5 copy.226
  373.2 4.1 multiply_reduce_fusion.2
  381.4 5.9 %convolution_convert_fusion.5 = bf16[768,768]{0,1:T(8,128)(2,1)} fusion(bf16[1664,768]{1,0:T(8,128)(2,1)} %copy-done.31, bf16[1664,768]{1,0:T(8,128)(2,1)} %bitcast.14), kind=kOutput, calls=%fused_computation.49 | convolution fusion | flops 1963524096 | bytes 6291456 | tf_op jit(solution)/shard_map/dot_general | solution.py:23
  387.3 3.7 all-to-all-start.5
  391.2 90.3 %reduce-scatter.10.cloned.1.call-done = bf16[24,3200]{1,0:T(8,128)(2,1)} async-done(((bf16[768,3200]{1,0:T(8,128)(2,1)}), bf16[24,3200]{1,0:T(8,128)(2,1)}) %reduce-scatter.10.cloned.1.call-update) | async-done | bytes 153616
  485.1 5.5 %convolution_bitcast_fusion = f32[1,768,768]{2,1,0:T(8,128)} fusion(bf16[1664,768]{1,0:T(8,128)(2,1)} %bitcast.6, bf16[1664,768]{1,0:T(8,128)(2,1)S(1)} %copy-done.12), kind=kOutput, calls=%fused_computation.47 | convolution fusion | flops 1962934272 | bytes 7471104 | tf_op jit(solution)/shard_map/dot_general | solution.py:23
  497.9 8.6 %all-gather.8.cloned.1.call-done = bf16[192,3200]{1,0:T(8,128)(2,1)} async-done(((bf16[24,3200]{1,0:T(8,128)(2,1)}), bf16[192,3200]{1,0:T(8,128)(2,1)}) %all-gather.8.cloned.1.call-update) | async-done | bytes 1228816 | tf_op jit(solution)/shard_map/all_gather | solution.py:388
  (235 shorter events, 88.2 us)
Async XLA Ops:
  7.2 210.0 %copy-start = (bf16[1,768,768]{2,1,0:T(8,128)(2,1)S(1)}, bf16[1,768,768]{2,1,0:T(8,128)(2,1)}, u32[]{:S(2)}) copy-start(bf16[1,768,768]{2,1,0:T(8,128)(2,1)} %param.29) | copy-start | bytes 3538948
  7.2 82.4 %all-gather.4.cloned.1.call-start = ((), (), s32[]{:S(2)}) async-start(), calls=%async_computation.9 | async-start | bytes 3852288 | tf_op jit(solution)/shard_map/all_gather | solution.py:109
  16.7 7.7 %copy-start.24 = (s32[2,65,2]{1,2,0:T(2,128)S(1)}, s32[2,65,2]{1,2,0:T(2,128)}, u32[]{:S(2)}) copy-start(s32[2,65,2]{1,2,0:T(2,128)} %param.19) | copy-start | bytes 3124
  16.7 7.8 %copy-start.30 = (s32[2]{0:T(128)S(1)}, s32[2]{0:T(128)}, u32[]{:S(2)}) copy-start(s32[2]{0:T(128)} %param.18) | copy-start | bytes 28
  16.7 8.0 %copy-start.3 = (f32[2,65,768]{2,0,1:T(2,128)S(1)}, f32[2,65,768]{2,0,1:T(2,128)}, u32[]{:S(2)}) copy-start(f32[2,65,768]{2,0,1:T(2,128)} %param.17) | copy-start | bytes 1198084
  17.9 8.7 %copy-start.23 = (f32[2,65,768]{2,0,1:T(2,128)S(1)}, f32[2,65,768]{2,0,1:T(2,128)}, u32[]{:S(2)}) copy-start(f32[2,65,768]{2,0,1:T(2,128)} %param.33) | copy-start | bytes 1198084
  17.9 158.5 %all-to-all-start.1 = ((bf16[4,768,192]{1,2,0:T(8,128)(2,1)}), bf16[4,768,192]{1,2,0:T(8,128)(2,1)}, u32[]{:S(2)}, u32[]{:S(2)}) async-start(bf16[4,768,192]{1,2,0:T(8,128)(2,1)} %copy.218), calls=%async_computation.1 | async-start | bytes 2359296 | tf_op jit(solution)/shard_map/all_to_all | solution.py:178
  24.4 120.7 %all-gather.6.cloned.1.call-start = ((), (), s32[]{:S(2)}) async-start(), calls=%async_computation.10 | async-start | bytes 1216512 | tf_op jit(solution)/shard_map/all_gather | solution.py:109
  25.7 67.4 %copy-start.25 = (f32[130]{0:T(256)}, f32[130]{0:T(256)S(1)}, u32[]{:S(2)}) copy-start(f32[130]{0:T(256)S(1)} %rsqrt.21) | copy-start | bytes 1564
  28.4 64.3 %copy-start.7 = (f32[130,768]{1,0:T(8,128)}, f32[130,768]{1,0:T(8,128)S(1)}, u32[]{:S(2)}) copy-start(f32[130,768]{1,0:T(8,128)S(1)} %reshape.269) | copy-start | bytes 1198084
  28.4 64.6 %copy-start.5 = (f32[130,768]{1,0:T(8,128)}, f32[130,768]{1,0:T(8,128)S(1)}, u32[]{:S(2)}) copy-start(f32[130,768]{1,0:T(8,128)S(1)} %reshape.266) | copy-start | bytes 1198084
  103.8 5.1 copy-start.9
  112.6 36.2 %copy-start.13 = (bf16[130,768]{1,0:T(8,128)(2,1)}, bf16[130,768]{1,0:T(8,128)(2,1)S(1)}, u32[]{:S(2)}) copy-start(bf16[130,768]{1,0:T(8,128)(2,1)S(1)} %reshape.268) | copy-start | bytes 599044
  176.4 35.9 %all-to-all-start = ((bf16[8,208,768]{2,1,0:T(8,128)(2,1)}), bf16[8,208,768]{2,1,0:T(8,128)(2,1)}, u32[]{:S(2)}, u32[]{:S(2)}) async-start(bf16[8,208,768]{2,1,0:T(8,128)(2,1)} %bitcast.102), calls=%async_computation | async-start | bytes 5111808 | tf_op jit(solution)/shard_map/all_to_all | solution.py:256
  212.3 4.5 copy-start.29
  212.3 4.8 copy-start.28
  212.3 36.1 %all-to-all-start.3 = ((bf16[8,208,768]{2,1,0:T(8,128)(2,1)}), bf16[8,208,768]{2,1,0:T(8,128)(2,1)}, u32[]{:S(2)}, u32[]{:S(2)}) async-start(bf16[8,208,768]{2,1,0:T(8,128)(2,1)} %bitcast.101), calls=%async_computation.4 | async-start | bytes 5111808 | tf_op jit(solution)/shard_map/all_to_all | solution.py:258
  248.4 36.1 %all-to-all-start.2 = ((bf16[8,208,768]{2,1,0:T(8,128)(2,1)}), bf16[8,208,768]{2,1,0:T(8,128)(2,1)}, u32[]{:S(2)}, u32[]{:S(2)}) async-start(bf16[8,208,768]{2,1,0:T(8,128)(2,1)} %bitcast.103), calls=%async_computation.2 | async-start | bytes 5111808 | tf_op jit(solution)/shard_map/all_to_all | solution.py:273
  284.5 35.9 %all-to-all-start.4 = ((bf16[8,208,768]{2,1,0:T(8,128)(2,1)}), bf16[8,208,768]{2,1,0:T(8,128)(2,1)}, u32[]{:S(2)}, u32[]{:S(2)}) async-start(bf16[8,208,768]{2,1,0:T(8,128)(2,1)} %bitcast.100), calls=%async_computation.5 | async-start | bytes 5111808 | tf_op jit(solution)/shard_map/all_to_all | solution.py:278
  288.9 38.9 %reduce-scatter.6.cloned.1.call-start = ((), (), s32[]{:S(2)}) async-start(), calls=%async_computation.11 | async-start | bytes 1290240 | tf_op jit(solution)/shard_map/reduce_scatter | solution.py:296
  299.9 53.8 %reduce-scatter.8.cloned.1.call-start = ((), (), s32[]{:S(2)}) async-start(), calls=%async_computation.12 | async-start | bytes 1105920 | tf_op jit(solution)/shard_map/reduce_scatter | solution.py:313
  325.2 28.5 %copy-start.22 = (bf16[128,768]{0,1:T(8,128)(2,1)S(1)}, bf16[128,768]{0,1:T(8,128)(2,1)}, u32[]{:S(2)}) copy-start(bf16[128,768]{0,1:T(8,128)(2,1)} %get-tuple-element.145) | copy-start | bytes 589828
  325.2 31.0 %copy-start.8 = (f32[130,768]{1,0:T(8,128)S(1)}, f32[130,768]{1,0:T(8,128)}, u32[]{:S(2)}) copy-start(f32[130,768]{1,0:T(8,128)} %copy-done.7) | copy-start | bytes 1198084
  325.3 156.3 %reduce-scatter.10.cloned.1.call-start = ((), (), s32[]{:S(2)}) async-start(), calls=%async_computation.14 | async-start | bytes 5068800
  359.8 4.5 copy-start.17
  361.0 5.4 %copy-start.14 = (bf16[130,768]{1,0:T(8,128)(2,1)S(1)}, bf16[130,768]{1,0:T(8,128)(2,1)}, u32[]{:S(2)}) copy-start(bf16[130,768]{1,0:T(8,128)(2,1)} %copy-done.13) | copy-start | bytes 599044
  362.3 6.0 %copy-start.18 = (bf16[2,12,64,65]{3,2,1,0:T(8,128)(2,1)S(1)}, bf16[2,12,64,65]{3,2,1,0:T(8,128)(2,1)}, u32[]{:S(2)}) copy-start(bf16[2,12,64,65]{3,2,1,0:T(8,128)(2,1)} %get-tuple-element.167) | copy-start | bytes 599044
  373.2 4.6 copy-start.19
  387.3 97.3 %copy-start.27 = (f32[768]{0:T(1024)S(1)}, f32[768]{0:T(1024)}, u32[]{:S(2)}) copy-start(f32[768]{0:T(1024)} %get-tuple-element.170) | copy-start | bytes 9220
  387.3 103.4 %all-to-all-start.5 = ((bf16[768,4,192]{0,2,1:T(8,128)(2,1)}), bf16[768,4,192]{0,2,1:T(8,128)(2,1)S(1)}, u32[]{:S(2)}, u32[]{:S(2)}) async-start(bf16[768,4,192]{0,2,1:T(8,128)(2,1)} %bitcast.27), calls=%async_computation.7 | async-start | bytes 2359296 | tf_op jit(solution)/shard_map/all_to_all | solution.py:281
  390.9 115.5 %all-gather.8.cloned.1.call-start = ((), (), s32[]{:S(2)}) async-start(), calls=%async_computation.13 | async-start | bytes 1382400 | tf_op jit(solution)/shard_map/all_gather | solution.py:388
  509.0 3.8 copy-start.1
  (12 other events, 31.4 us)
Sparse Core Ops, SparseCore 0:
  14.1 75.4 all-gather.3
  92.5 52.5 all-gather.5
  300.0 27.7 reduce-scatter.5
  330.5 23.1 reduce-scatter.7
  381.5 99.9 reduce-scatter.9
  483.3 23.1 all-gather.7
